TPU v7x, 32 devices: a whole 2x2x4 slice. The times are simulated.
32 devices in a mesh: row: 4 (over z), col: 8 (over y, x, core).
Axes of the slice: x: 2, y: 2, z: 4, core: 2. Of those that a mesh axis runs over, the one named last changes fastest.
Arguments:
- hessian: float32 [16384, 4, 8, 512], P('row', None, 'col'), may hold values from -1 to 16, as said below
- weights: bfloat16 [512, 16384], P('col', 'row'), may hold values from -6 to 6
- codes: int32 [512, 8192], P('col', 'row'), may hold values from 0 to 255
- tile_map: int32 [32, 64], P('col', 'row'), may hold values from 0 to 511
- codebooks: float32 [512, 2, 256], replicated, may hold values from -6 to 6
Outputs:
- adjusted_codebooks: float32 [512, 2, 256], replicated
Inputs may be any that keep to these rules, and one draw needn't show every extreme that they name: `hessian`: H is symmetric with a dominant positive diagonal.
All inputs are finite; a program needn't handle non-finite values.
Results may differ from a plain program's by a relative error of at most 0.0003.
Values sent between devices are 32-bit elements; how exact they have to be, the bound alone decides.
A program may use at most 192 MiB of HBM per device.

v0:
```python
import jax
import jax.numpy as jnp
from jax import lax
from jax.sharding import PartitionSpec as P

CODES = 256
NB = 512
TILE_ROWS = 16
TILE_COLS = 256
STEPS = 2
learn_rate = 0.01


def per_device(hessian, weights, codes, tile_map, codebooks):
    rows_local, cols_local = weights.shape
    rows_tiles = rows_local // TILE_ROWS
    cols_tiles = cols_local // TILE_COLS
    tile_count = rows_tiles * cols_tiles
    half_width = TILE_COLS // 2
    pair_count = TILE_ROWS * half_width
    hessian_tile = hessian.reshape(
        hessian.shape[0], hessian.shape[1] * hessian.shape[2] * hessian.shape[3]
    )
    code_tiles = (
        codes.reshape(rows_tiles, TILE_ROWS, cols_tiles, half_width)
        .transpose(0, 2, 1, 3)
        .reshape(tile_count, pair_count)
    )
    code_onehot = (
        code_tiles[:, :, None] == lax.broadcasted_iota(jnp.int32, (1, 1, CODES), 2)
    ).astype(jnp.float32)
    book_onehot = (
        tile_map.reshape(-1)[:, None] == lax.broadcasted_iota(jnp.int32, (1, NB), 1)
    ).astype(jnp.float32)
    for iteration in range(STEPS):
        tile_books = jnp.einsum(
            "tb,bck->tck", book_onehot, codebooks, precision=lax.Precision.HIGHEST
        )
        rebuilt_tiles = jnp.einsum(
            "tpk,tck->tpc", code_onehot, tile_books, precision=lax.Precision.HIGHEST
        )
        rebuilt = (
            rebuilt_tiles.reshape(rows_tiles, cols_tiles, TILE_ROWS, half_width, 2)
            .transpose(0, 2, 1, 3, 4)
            .reshape(rows_local, cols_local)
        )
        error = rebuilt - weights.astype(jnp.float32)
        error_piece = lax.all_to_all(error, "col", split_axis=1, concat_axis=0, tiled=True)
        error_spread = lax.all_gather(error_piece, "row", axis=1, tiled=True)
        weight_grad = 2.0 * lax.psum_scatter(
            lax.dot_general(
                error_spread,
                hessian_tile,
                (((1,), (1,)), ((), ())),
                precision=lax.Precision.HIGHEST,
                preferred_element_type=jnp.float32,
            ),
            "col",
            scatter_dimension=0,
            tiled=True,
        )
        grad_tiles = (
            weight_grad.reshape(rows_tiles, TILE_ROWS, cols_tiles, half_width, 2)
            .transpose(0, 2, 1, 3, 4)
            .reshape(tile_count, pair_count, 2)
        )
        tile_grads = jnp.einsum(
            "tpk,tpc->tck", code_onehot, grad_tiles, precision=lax.Precision.HIGHEST
        )
        local_grad = jnp.einsum(
            "tb,tck->bck", book_onehot, tile_grads, precision=lax.Precision.HIGHEST
        )
        total_even, total_odd = lax.psum((local_grad[:, 0, :], local_grad[:, 1, :]), ("row", "col"))
        book_grad = jnp.stack([total_even, total_odd], axis=1)
        codebooks = codebooks - learn_rate * book_grad
    return codebooks


def solution(mesh):
    placed = (P("row", None, "col", None), P("col", "row"), P("col", "row"), P("col", "row"), P())
    return jax.shard_map(per_device, mesh=mesh, in_specs=placed, out_specs=P(), check_vma=False)
```

profile of v0, /device:TPU:0, one launch (start us, length us, event | category | flops | bytes accessed | tf_op | source)
XLA Modules:
  0.0 1101.7 jit_solution(13116930296548509444)
XLA Ops:
  6.5 0.0 all-gather.3.cloned.1.call-start
  6.5 0.8 eq.30
  7.3 1.1 copy.32
  8.4 0.2 copy.10
  8.6 0.2 copy.51
  8.8 2.0 fusion.10
  10.7 0.0 copy-done.4
  10.8 0.0 copy-start.3
  10.8 68.2 %fusion.3 = f32[64,2048,2]{1,2,0:T(2,128)S(1)} fusion(s32[64,2048]{1,0:T(8,128)S(1)} %bitcast.70, f32[64,2,256]{2,0,1:T(8,128)S(1)} %fusion.10), kind=kOutput, calls=%fused_computation.4 | convolution fusion | flops 838860800 | bytes 1703936 | tf_op jit(solution)/shard_map/tpk,tck->tpc/dot_general | solution.py:39
  79.0 0.8 reshape.39
  79.8 0.5 copy.12
  80.3 5.8 copy.11
  86.1 6.5 reshape.40
  92.6 1.5 convert_subtract_fusion.1
  94.2 2.2 copy.13
  96.3 20.4 %all_to_all.38 = f32[64,8,512]{2,0,1:T(8,128)} all-to-all(f32[64,8,512]{2,0,1:T(8,128)S(1)} %copy.13), channel_id=1, replica_groups=mesh['row'=4,'col'=8] {'col'}, dimensions={1} | all-to-all | bytes 2097152 | tf_op jit(solution)/shard_map/all_to_all | solution.py:48
  116.8 0.0 all-gather.3.cloned.1.call-update
  116.8 0.2 reduce-scatter.3.cloned.1.call-start
  117.0 101.8 %reduce = f32[4096,4,512]{2,1,0:T(4,128)} reduce(f32[4096,4,1,512]{3,2,1,0:T(1,128)} %param.5, f32[]{:T(128)} %constant.6), dimensions={2}, to_apply=%param.5.reduce_sub_computation | reduce | bytes 67108864 | tf_op args[0]
  218.8 29.9 %copy.34 = f32[512,8,4,512]{3,1,2,0:T(8,128)} copy(f32[512,8,4,512]{3,2,1,0:T(4,128)} %bitcast.56) | data formatting | bytes 67108864
  248.7 59.3 %fusion.33 = f32[512,4096]{1,0:T(8,128)} fusion(f32[512,2048]{1,0:T(8,128)} %all-gather.3.cloned.1.call-done, f32[4096,2048]{1,0:T(8,128)} %bitcast.61), kind=kOutput, calls=%fused_computation.37 | convolution fusion | flops 51539607552 | bytes 46137344 | tf_op jit(solution)/shard_map/dot_general | solution.py:51
  308.0 0.0 reduce-scatter.3.cloned.1.call-update
  308.1 0.0 all-reduce.7.cloned.1.call-start
  308.1 71.0 %reduce-scatter.3.cloned.1.call-done = f32[64,4096]{1,0:T(8,128)} async-done(((f32[512,4096]{1,0:T(8,128)}), f32[64,4096]{1,0:T(8,128)}) %reduce-scatter.3.cloned.1.call-update) | async-done | bytes 1048592 | tf_op jit(solution)/shard_map/reduce_scatter | solution.py:50
  379.1 2.3 broadcast_multiply_fusion.1
  381.4 1.8 copy.14
  383.2 5.5 reshape.42
  388.7 6.7 copy.28
  395.4 0.6 reshape.53
  395.9 0.0 copy-start
  395.9 46.3 %fusion.2 = f32[64,2,256]{2,1,0:T(2,128)S(1)} fusion(f32[64,2048,2]{1,2,0:T(2,128)S(1)} %reshape.53, s32[64,2048]{1,0:T(8,128)} %bitcast.71), kind=kOutput, calls=%fused_computation.3 | convolution fusion | flops 838860800 | bytes 1703936 | tf_op jit(solution)/shard_map/tpk,tpc->tck/dot_general | solution.py:67
  442.2 0.7 fusion.17
  442.9 1.0 fusion.32
  443.9 0.0 all-reduce.7.cloned.1.call-update
  444.0 0.3 all-gather.5.cloned.1.call-start
  444.2 131.0 %all-reduce.7.cloned.1.call-done = (f32[512,1,256]{2,0,1:T(8,128)}, f32[512,1,256]{2,0,1:T(8,128)}) async-done(((f32[512,1,256]{2,0,1:T(8,128)}, f32[512,1,256]{2,0,1:T(8,128)}), (f32[512,1,256]{2,0,1:T(8,128)}, f32[512,1,256]{2,0,1:T(8,128)})) %all-reduce.7.cloned.1.call-update) | async-done | bytes 1048592 | tf_op jit(solution)/shard_map/psum | solution.py:73
  575.2 0.0 copy-done
  575.2 1.8 fusion.12
  577.0 69.8 %fusion.1 = f32[64,2048,2]{1,2,0:T(2,128)} fusion(s32[64,2048]{1,0:T(8,128)} %bitcast.72, f32[64,2,256]{2,0,1:T(8,128)S(1)} %fusion.12), kind=kOutput, calls=%fused_computation.2 | convolution fusion | flops 838860800 | bytes 1703936 | tf_op jit(solution)/shard_map/tpk,tck->tpc/dot_general | solution.py:39
  646.8 2.1 reshape.44
  648.8 5.8 copy.17
  654.6 7.6 reshape.45
  662.2 3.1 convert_subtract_fusion
  665.4 2.2 copy.18
  667.6 18.8 %all_to_all.39 = f32[64,8,512]{2,0,1:T(8,128)} all-to-all(f32[64,8,512]{2,0,1:T(8,128)S(1)} %copy.18), channel_id=1, replica_groups=mesh['row'=4,'col'=8] {'col'}, dimensions={1} | all-to-all | bytes 2097152 | tf_op jit(solution)/shard_map/all_to_all | solution.py:48
  686.4 0.0 all-gather.5.cloned.1.call-update
  686.4 0.0 reduce-scatter.5.cloned.1.call-start
  686.5 78.5 %all-gather.5.cloned.1.call-done = f32[512,2048]{1,0:T(8,128)} async-done(((f32[512,512]{1,0:T(8,128)}), f32[512,2048]{1,0:T(8,128)}) %all-gather.5.cloned.1.call-update) | async-done | bytes 4194320 | tf_op jit(solution)/shard_map/all_gather | solution.py:49
  764.9 59.3 %fusion.34 = f32[512,4096]{1,0:T(8,128)} fusion(f32[512,2048]{1,0:T(8,128)} %all-gather.5.cloned.1.call-done, f32[4096,2048]{1,0:T(8,128)} %bitcast.62), kind=kOutput, calls=%fused_computation.38 | convolution fusion | flops 51539607552 | bytes 46137344 | tf_op jit(solution)/shard_map/dot_general | solution.py:51
  824.2 0.0 reduce-scatter.5.cloned.1.call-update
  824.3 0.3 all-reduce.5.cloned.1.call-start
  824.6 69.8 %reduce-scatter.5.cloned.1.call-done = f32[64,4096]{1,0:T(8,128)} async-done(((f32[512,4096]{1,0:T(8,128)}), f32[64,4096]{1,0:T(8,128)}) %reduce-scatter.5.cloned.1.call-update) | async-done | bytes 1048592 | tf_op jit(solution)/shard_map/reduce_scatter | solution.py:50
  894.4 1.3 broadcast_multiply_fusion
  895.7 2.0 copy.19
  897.7 7.3 reshape.46
  905.0 6.7 copy.29
  911.6 0.6 reshape.54
  912.2 46.3 %fusion = f32[64,2,256]{2,1,0:T(2,128)S(1)} fusion(f32[64,2048,2]{1,2,0:T(2,128)S(1)} %reshape.54, s32[64,2048]{1,0:T(8,128)} %bitcast.73), kind=kOutput, calls=%fused_computation.1 | convolution fusion | flops 838860800 | bytes 1703936 | tf_op jit(solution)/shard_map/tpk,tpc->tck/dot_general | solution.py:67
  958.5 0.7 fusion.14
  959.2 1.1 fusion.31
  960.2 0.0 all-reduce.5.cloned.1.call-update
  960.3 131.3 %all-reduce.5.cloned.1.call-done = (f32[512,1,256]{2,0,1:T(8,128)}, f32[512,1,256]{2,0,1:T(8,128)}) async-done(((f32[512,1,256]{2,0,1:T(8,128)}, f32[512,1,256]{2,0,1:T(8,128)}), (f32[512,1,256]{2,0,1:T(8,128)}, f32[512,1,256]{2,0,1:T(8,128)})) %all-reduce.5.cloned.1.call-update) | async-done | bytes 1048592 | tf_op jit(solution)/shard_map/psum | solution.py:73
  1091.6 1.4 fusion.9
  1093.0 1.8 copy.21
  (7 shorter events, 0.0 us)
Async XLA Ops:
  6.5 242.2 %all-gather.3.cloned.1.call-start = ((), (), s32[]{:S(2)}) async-start(), calls=%async_computation.4 | async-start | bytes 5242880 | tf_op jit(solution)/shard_map/all_gather | solution.py:49
  8.8 2.0 copy-start.4
  10.8 69.1 %copy-start.3 = (bf16[64,4096]{1,0:T(8,128)(2,1)S(1)}, bf16[64,4096]{1,0:T(8,128)(2,1)}, u32[]{:S(2)}) copy-start(bf16[64,4096]{1,0:T(8,128)(2,1)} %param.6) | copy-start | bytes 1572868
  116.8 262.3 %reduce-scatter.3.cloned.1.call-start = ((), (), s32[]{:S(2)}) async-start(), calls=%async_computation.5 | async-start | bytes 9437184 | tf_op jit(solution)/shard_map/reduce_scatter | solution.py:50
  308.1 267.1 %all-reduce.7.cloned.1.call-start = ((), (), s32[]{:S(2)}) async-start(), calls=%async_computation.9 | async-start | bytes 2097152 | tf_op jit(solution)/shard_map/psum | solution.py:73
  395.9 179.3 %copy-start = (f32[512,2,256]{2,1,0:T(2,128)S(1)}, f32[512,2,256]{2,1,0:T(2,128)}, u32[]{:S(2)}) copy-start(f32[512,2,256]{2,1,0:T(2,128)} %param.9) | copy-start | bytes 3145732
  444.0 321.0 %all-gather.5.cloned.1.call-start = ((), (), s32[]{:S(2)}) async-start(), calls=%async_computation.6 | async-start | bytes 5242880 | tf_op jit(solution)/shard_map/all_gather | solution.py:49
  686.4 208.0 %reduce-scatter.5.cloned.1.call-start = ((), (), s32[]{:S(2)}) async-start(), calls=%async_computation.7 | async-start | bytes 9437184 | tf_op jit(solution)/shard_map/reduce_scatter | solution.py:50
  824.3 267.3 %all-reduce.5.cloned.1.call-start = ((), (), s32[]{:S(2)}) async-start(), calls=%async_computation.8 | async-start | bytes 2097152 | tf_op jit(solution)/shard_map/psum | solution.py:73
  912.2 179.4 %copy-start.1 = (f32[512,1,256]{2,0,1:T(8,128)S(1)}, f32[512,1,256]{2,0,1:T(8,128)}, u32[]{:S(2)}) copy-start(f32[512,1,256]{2,0,1:T(8,128)} %get-tuple-element.7) | copy-start | bytes 1572868
  912.2 179.4 %copy-start.2 = (f32[512,1,256]{2,0,1:T(8,128)S(1)}, f32[512,1,256]{2,0,1:T(8,128)}, u32[]{:S(2)}) copy-start(f32[512,1,256]{2,0,1:T(8,128)} %get-tuple-element.8) | copy-start | bytes 1572868
Sparse Core Ops, SparseCore 0:
  116.9 80.0 all-gather.2
  308.2 70.8 reduce-scatter.2
  444.1 131.0 all-reduce.6
  686.5 78.3 all-gather.4
  824.4 69.9 reduce-scatter.4
  960.4 131.1 all-reduce.4
where the time goes:
time: 1100 us
  waiting for transfers between devices  482 us (44%)
  matrix products  354 us (32%)
  other arithmetic  111 us (10%)
  local copies, waits for them, and re-layouts  100 us (9%)
  blocking collectives  39.3 us (4%)
  between operations  13.7 us (1%)
    psum x2, waiting for transfers between devices, per_device(): lax.psum((local_grad[:, 0, :], local_grad[:, 1, :]), ('row', 'col'))  262 us
    reduce_scatter x2, waiting for transfers between devices, per_device(): lax.psum_scatter(lax.dot_general(error_spread, hessian_tile, (((1,), (1,)...  141 us
    dot_general x2, matrix products, per_device(): jnp.einsum('tpk,tck->tpc', code_onehot, tile_books, precision=lax.Precisi...  138 us
    dot_general x2, matrix products, per_device(): lax.dot_general(error_spread, hessian_tile, (((1,), (1,)), ((), ())), pre...  119 us
    unnamed x1, other arithmetic  102 us
    dot_general x2, matrix products, per_device(): jnp.einsum('tpk,tpc->tck', code_onehot, grad_tiles, precision=lax.Precisi...  92.5 us
    all_gather x2, waiting for transfers between devices, per_device(): error_spread = lax.all_gather(error_piece, 'row', axis=1, tiled=True)  78.5 us
    all_to_all x2, blocking collectives, per_device(): lax.all_to_all(error, 'col', split_axis=1, concat_axis=0, tiled=True)  39.3 us
  transfers between devices with their start and end apart: 6, of which 5 were waited for; matrix products, arithmetic and copies ran while one was open for 12% of the time, Pallas kernels for 0%

commit v1 on v0

--- a/solution.py
+++ b/solution.py
@@ -46,7 +46,8 @@
         )
         error = rebuilt - weights.astype(jnp.float32)
         error_piece = lax.all_to_all(error, "col", split_axis=1, concat_axis=0, tiled=True)
-        error_spread = lax.all_gather(error_piece, "row", axis=1, tiled=True)
+        parts = lax.all_gather(error_piece, "row")
+        error_spread = jnp.concatenate(parts, axis=1)
         weight_grad = 2.0 * lax.psum_scatter(
             lax.dot_general(
                 error_spread,

time: 1100 us -> 1220 us (1.11)
  matrix products: 354 us -> 459 us
    dot_general x2, matrix products: 119 us -> 223 us  [per_device(): lax.dot_general(error_spread, hessian_tile, (((1,), (1,)), ((), ())), pre...]
  transfers between devices with their start and end apart: 6 -> 6, of which waited for: 5 -> 5; matrix products, arithmetic and copies ran while one was open for 12% -> 11% of each run, Pallas kernels for 0% -> 0%
where the time goes in v1:
time: 1220 us
  waiting for transfers between devices  482 us (40%)
  matrix products  459 us (38%)
  local copies, waits for them, and re-layouts  111 us (9%)
  other arithmetic  111 us (9%)
  blocking collectives  39.3 us (3%)
  between operations  13.9 us (1%)
    psum x2, waiting for transfers between devices, per_device(): lax.psum((local_grad[:, 0, :], local_grad[:, 1, :]), ('row', 'col'))  263 us
    dot_general x2, matrix products, per_device(): lax.dot_general(error_spread, hessian_tile, (((1,), (1,)), ((), ())), pre...  223 us
    reduce_scatter x2, waiting for transfers between devices, per_device(): lax.psum_scatter(lax.dot_general(error_spread, hessian_tile, (((1,), (1,)...  141 us
    dot_general x2, matrix products, per_device(): jnp.einsum('tpk,tck->tpc', code_onehot, tile_books, precision=lax.Precisi...  138 us
    unnamed x1, other arithmetic  102 us
    dot_general x2, matrix products, per_device(): jnp.einsum('tpk,tpc->tck', code_onehot, grad_tiles, precision=lax.Precisi...  92.5 us
    all_gather x2, waiting for transfers between devices, per_device(): parts = lax.all_gather(error_piece, 'row')  78.5 us
    all_to_all x2, blocking collectives, per_device(): lax.all_to_all(error, 'col', split_axis=1, concat_axis=0, tiled=True)  39.3 us
  transfers between devices with their start and end apart: 6, of which 5 were waited for; matrix products, arithmetic and copies ran while one was open for 11% of the time, Pallas kernels for 0%

profile of v1, /device:TPU:0, one launch (start us, length us, event | category | flops | bytes accessed | tf_op | source)
XLA Modules:
  0.0 1217.0 jit_solution(11886295043134093151)
XLA Ops:
  6.5 0.8 eq.30
  7.3 1.1 copy.49
  8.4 0.2 copy.24
  8.6 0.2 copy.68
  8.8 2.0 fusion.10
  10.7 0.0 copy-done.4
  10.8 0.0 copy-start.3
  10.8 68.2 %fusion.3 = f32[64,2048,2]{1,2,0:T(2,128)S(1)} fusion(s32[64,2048]{1,0:T(8,128)S(1)} %bitcast.78, f32[64,2,256]{2,0,1:T(8,128)S(1)} %fusion.10), kind=kOutput, calls=%fused_computation.4 | convolution fusion | flops 838860800 | bytes 1703936 | tf_op jit(solution)/shard_map/tpk,tck->tpc/dot_general | solution.py:39
  79.0 0.8 reshape.53
  79.8 0.5 copy.28
  80.3 5.8 copy.27
  86.1 6.5 reshape.54
  92.6 1.5 convert_subtract_fusion.1
  94.2 2.2 copy.29
  96.3 20.4 %all_to_all.32 = f32[64,8,512]{2,0,1:T(8,128)} all-to-all(f32[64,8,512]{2,0,1:T(8,128)S(1)} %copy.29), channel_id=1, replica_groups=mesh['row'=4,'col'=8] {'col'}, dimensions={1} | all-to-all | bytes 2097152 | tf_op jit(solution)/shard_map/all_to_all | solution.py:48
  116.8 0.0 all-gather.3.cloned.1.call-update
  116.8 0.0 reduce-scatter.3.cloned.1.call-start
  116.8 101.8 %reduce = f32[4096,4,512]{2,1,0:T(4,128)} reduce(f32[4096,4,1,512]{3,2,1,0:T(1,128)} %param.5, f32[]{:T(128)} %constant.6), dimensions={2}, to_apply=%param.5.reduce_sub_computation | reduce | bytes 67108864 | tf_op args[0]
  218.6 29.9 %copy.51 = f32[512,8,4,512]{3,1,2,0:T(8,128)} copy(f32[512,8,4,512]{3,2,1,0:T(4,128)} %bitcast.62) | data formatting | bytes 67108864
  248.6 5.2 copy.30
  253.8 111.6 %fusion.33 = f32[512,4096]{1,0:T(8,128)} fusion(f32[512,2048]{0,1:T(8,128)} %bitcast.72, f32[4096,2048]{1,0:T(8,128)} %bitcast.67), kind=kOutput, calls=%fused_computation.37 | convolution fusion | flops 51539607552 | bytes 46137344 | tf_op jit(solution)/shard_map/dot_general | solution.py:52
  365.4 0.0 reduce-scatter.3.cloned.1.call-update
  365.4 0.0 all-reduce.7.cloned.1.call-start
  365.5 71.0 %reduce-scatter.3.cloned.1.call-done = f32[64,4096]{1,0:T(8,128)} async-done(((f32[512,4096]{1,0:T(8,128)}), f32[64,4096]{1,0:T(8,128)}) %reduce-scatter.3.cloned.1.call-update) | async-done | bytes 1048592 | tf_op jit(solution)/shard_map/reduce_scatter | solution.py:51
  436.5 2.3 broadcast_multiply_fusion.1
  438.7 1.8 copy.31
  440.6 5.5 reshape.58
  446.1 6.7 copy.45
  452.7 0.6 reshape.71
  453.3 0.0 copy-start
  453.3 46.3 %fusion.2 = f32[64,2,256]{2,1,0:T(2,128)S(1)} fusion(f32[64,2048,2]{1,2,0:T(2,128)S(1)} %reshape.71, s32[64,2048]{1,0:T(8,128)} %bitcast.79), kind=kOutput, calls=%fused_computation.3 | convolution fusion | flops 838860800 | bytes 1703936 | tf_op jit(solution)/shard_map/tpk,tpc->tck/dot_general | solution.py:68
  499.6 0.7 fusion.17
  500.3 1.0 fusion.32
  501.3 0.0 all-reduce.7.cloned.1.call-update
  501.3 0.0 all-gather.5.cloned.1.call-start
  501.4 131.3 %all-reduce.7.cloned.1.call-done = (f32[512,1,256]{2,0,1:T(8,128)}, f32[512,1,256]{2,0,1:T(8,128)}) async-done(((f32[512,1,256]{2,0,1:T(8,128)}, f32[512,1,256]{2,0,1:T(8,128)}), (f32[512,1,256]{2,0,1:T(8,128)}, f32[512,1,256]{2,0,1:T(8,128)})) %all-reduce.7.cloned.1.call-update) | async-done | bytes 1048592 | tf_op jit(solution)/shard_map/psum | solution.py:74
  632.7 1.8 fusion.12
  634.5 69.8 %fusion.1 = f32[64,2048,2]{1,2,0:T(2,128)} fusion(s32[64,2048]{1,0:T(8,128)} %bitcast.80, f32[64,2,256]{2,0,1:T(8,128)S(1)} %fusion.12), kind=kOutput, calls=%fused_computation.2 | convolution fusion | flops 838860800 | bytes 1703936 | tf_op jit(solution)/shard_map/tpk,tck->tpc/dot_general | solution.py:39
  704.2 2.1 reshape.60
  706.3 5.8 copy.37
  712.1 7.6 reshape.61
  719.7 3.1 convert_subtract_fusion
  722.8 2.2 copy.38
  725.0 18.8 %all_to_all.33 = f32[64,8,512]{2,0,1:T(8,128)} all-to-all(f32[64,8,512]{2,0,1:T(8,128)S(1)} %copy.38), channel_id=1, replica_groups=mesh['row'=4,'col'=8] {'col'}, dimensions={1} | all-to-all | bytes 2097152 | tf_op jit(solution)/shard_map/all_to_all | solution.py:48
  743.8 0.0 all-gather.5.cloned.1.call-update
  743.8 0.0 reduce-scatter.5.cloned.1.call-start
  743.9 78.5 %all-gather.5.cloned.1.call-done = f32[4,512,512]{2,1,0:T(8,128)} async-done(((f32[1,512,512]{2,1,0:T(8,128)}), f32[4,512,512]{2,1,0:T(8,128)}) %all-gather.5.cloned.1.call-update) | async-done | bytes 4194320 | tf_op jit(solution)/shard_map/all_gather | solution.py:49
  822.4 5.2 copy.39
  827.6 111.8 %fusion.34 = f32[512,4096]{1,0:T(8,128)} fusion(f32[512,2048]{0,1:T(8,128)} %bitcast.71, f32[4096,2048]{1,0:T(8,128)} %bitcast.68), kind=kOutput, calls=%fused_computation.38 | convolution fusion | flops 51539607552 | bytes 46137344 | tf_op jit(solution)/shard_map/dot_general | solution.py:52
  939.4 0.0 reduce-scatter.5.cloned.1.call-update
  939.5 0.0 all-reduce.5.cloned.1.call-start
  939.5 70.1 %reduce-scatter.5.cloned.1.call-done = f32[64,4096]{1,0:T(8,128)} async-done(((f32[512,4096]{1,0:T(8,128)}), f32[64,4096]{1,0:T(8,128)}) %reduce-scatter.5.cloned.1.call-update) | async-done | bytes 1048592 | tf_op jit(solution)/shard_map/reduce_scatter | solution.py:51
  1009.6 1.3 broadcast_multiply_fusion
  1010.9 2.0 copy.40
  1012.9 7.3 reshape.64
  1020.2 6.7 copy.46
  1026.8 0.6 reshape.72
  1027.4 46.3 %fusion = f32[64,2,256]{2,1,0:T(2,128)S(1)} fusion(f32[64,2048,2]{1,2,0:T(2,128)S(1)} %reshape.72, s32[64,2048]{1,0:T(8,128)} %bitcast.81), kind=kOutput, calls=%fused_computation.1 | convolution fusion | flops 838860800 | bytes 1703936 | tf_op jit(solution)/shard_map/tpk,tpc->tck/dot_general | solution.py:68
  1073.7 0.7 fusion.14
  1074.4 1.1 fusion.31
  1075.4 0.0 all-reduce.5.cloned.1.call-update
  1075.5 131.3 %all-reduce.5.cloned.1.call-done = (f32[512,1,256]{2,0,1:T(8,128)}, f32[512,1,256]{2,0,1:T(8,128)}) async-done(((f32[512,1,256]{2,0,1:T(8,128)}, f32[512,1,256]{2,0,1:T(8,128)}), (f32[512,1,256]{2,0,1:T(8,128)}, f32[512,1,256]{2,0,1:T(8,128)})) %all-reduce.5.cloned.1.call-update) | async-done | bytes 1048592 | tf_op jit(solution)/shard_map/psum | solution.py:74
  1206.8 1.4 fusion.9
  1208.2 1.8 copy.44
  (9 shorter events, 0.0 us)
Async XLA Ops:
  6.5 242.0 %all-gather.3.cloned.1.call-start = ((), (), s32[]{:S(2)}) async-start(), calls=%async_computation.4 | async-start | bytes 5242880 | tf_op jit(solution)/shard_map/all_gather | solution.py:49
  8.8 2.0 copy-start.4
  10.8 69.1 %copy-start.3 = (bf16[64,4096]{1,0:T(8,128)(2,1)S(1)}, bf16[64,4096]{1,0:T(8,128)(2,1)}, u32[]{:S(2)}) copy-start(bf16[64,4096]{1,0:T(8,128)(2,1)} %param.6) | copy-start | bytes 1572868
  116.8 319.7 %reduce-scatter.3.cloned.1.call-start = ((), (), s32[]{:S(2)}) async-start(), calls=%async_computation.5 | async-start | bytes 9437184 | tf_op jit(solution)/shard_map/reduce_scatter | solution.py:51
  365.4 267.2 %all-reduce.7.cloned.1.call-start = ((), (), s32[]{:S(2)}) async-start(), calls=%async_computation.9 | async-start | bytes 2097152 | tf_op jit(solution)/shard_map/psum | solution.py:74
  453.3 179.4 %copy-start = (f32[512,2,256]{2,1,0:T(2,128)S(1)}, f32[512,2,256]{2,1,0:T(2,128)}, u32[]{:S(2)}) copy-start(f32[512,2,256]{2,1,0:T(2,128)} %param.9) | copy-start | bytes 3145732
  501.3 321.1 %all-gather.5.cloned.1.call-start = ((), (), s32[]{:S(2)}) async-start(), calls=%async_computation.6 | async-start | bytes 5242880 | tf_op jit(solution)/shard_map/all_gather | solution.py:49
  743.8 265.8 %reduce-scatter.5.cloned.1.call-start = ((), (), s32[]{:S(2)}) async-start(), calls=%async_computation.7 | async-start | bytes 9437184 | tf_op jit(solution)/shard_map/reduce_scatter | solution.py:51
  939.5 267.3 %all-reduce.5.cloned.1.call-start = ((), (), s32[]{:S(2)}) async-start(), calls=%async_computation.8 | async-start | bytes 2097152 | tf_op jit(solution)/shard_map/psum | solution.py:74
  1027.4 179.4 %copy-start.1 = (f32[512,1,256]{2,0,1:T(8,128)S(1)}, f32[512,1,256]{2,0,1:T(8,128)}, u32[]{:S(2)}) copy-start(f32[512,1,256]{2,0,1:T(8,128)} %get-tuple-element.7) | copy-start | bytes 1572868
  1027.4 179.4 %copy-start.2 = (f32[512,1,256]{2,0,1:T(8,128)S(1)}, f32[512,1,256]{2,0,1:T(8,128)}, u32[]{:S(2)}) copy-start(f32[512,1,256]{2,0,1:T(8,128)} %get-tuple-element.8) | copy-start | bytes 1572868
Sparse Core Ops, SparseCore 0:
  116.9 80.0 all-gather.2
  365.6 70.8 reduce-scatter.2
  501.4 131.1 all-reduce.6
  744.0 78.3 all-gather.4
  939.6 69.9 reduce-scatter.4
  1075.6 131.1 all-reduce.4
